TPU v7x, 32 devices: a whole 2x2x4 slice. The times are simulated.
32 devices in a mesh: row: 2 (over x), col: 16 (over z, y, core).
Axes of the slice: x: 2, y: 2, z: 4, core: 2. Of those that a mesh axis runs over, the one named last changes fastest.
Arguments:
- query_proj: bfloat16 [16384, 4096], P(('col', 'row')), may hold values from -9 to 9
- key_proj: bfloat16 [16384, 512], P(('col', 'row')), may hold values from -9 to 9
- value_proj: bfloat16 [16384, 512], P(('col', 'row')), may hold values from -6 to 6
- segment_ids: int32 [16, 1024], P('col'), may hold values from 0 to 3, never falling along the last dimension, each value on 1 to 512 neighbouring positions
- out_weight: bfloat16 [4096, 8192], P('col', 'row'), may hold values from -0.09375 to 0.09375
- residual: bfloat16 [16384, 8192], P('col', 'row'), may hold values from -4 to 4
- norm_gain: float32 [8192], P('row'), may hold values from 0.1 to 1.9
Outputs:
- residual_sum: bfloat16 [16384, 8192], P('col', 'row')
- normed: bfloat16 [16384, 8192], P('col', 'row')
Inputs may be any that keep to these rules, and one draw needn't show every extreme that they name: `segment_ids`: along each packed sequence the document number never falls; each document spans at most 512 positions and one spans exactly that.
All inputs are finite; a program needn't handle non-finite values.
Results may differ from a plain program's by a relative error of at most 0.0044.
Values may be sent and summed in bfloat16 or wider, within the bound.
A program may use at most 192 MiB of HBM per device.

v0:
```python
import jax
import jax.numpy as jnp
from jax import lax
from jax.sharding import PartitionSpec as P

D = 8192
HD = 128
HK = 4


def attend_local(query_heads, key_heads, value_heads, segment_row):
    length = query_heads.shape[0]
    kv_local = key_heads.shape[1] // HD
    group = query_heads.shape[1] // HD // kv_local
    query_grid = query_heads.reshape(length, kv_local, group, HD).transpose(1, 2, 0, 3)
    key_grid = key_heads.reshape(length, kv_local, HD).transpose(1, 0, 2)
    value_grid = value_heads.reshape(length, kv_local, HD).transpose(1, 0, 2)
    places = jnp.arange(length)
    allowed = (segment_row[:, None] == segment_row[None, :]) & (places[None, :] <= places[:, None])

    def one_group(operands):
        group_query, group_key, group_value = operands
        scores = jnp.einsum(
            "gqd,kd->gqk", group_query, group_key, preferred_element_type=jnp.float32
        ) * HD ** (-0.5)
        scores = jnp.where(allowed, scores, jnp.float32(-1e30))
        peak = jnp.max(scores, axis=-1, keepdims=True)
        weights = jnp.where(allowed, jnp.exp(scores - peak), jnp.float32(0.0))
        totals = jnp.sum(weights, axis=-1, keepdims=True)
        probs = weights.astype(jnp.bfloat16)
        mixture = (
            jnp.einsum("gqk,kd->gqd", probs, group_value, preferred_element_type=jnp.float32)
            / totals
        )
        return mixture.astype(jnp.bfloat16)

    heads_out = lax.map(one_group, (query_grid, key_grid, value_grid))
    return heads_out.transpose(2, 0, 1, 3).reshape(length, kv_local * group * HD)


def widen_heads(proj_rows, repeat):
    rows_local = proj_rows.shape[0]
    kv_count = proj_rows.shape[1] // HD
    if repeat == 1:
        return proj_rows
    spread = jnp.broadcast_to(
        proj_rows.reshape(rows_local, kv_count, 1, HD), (rows_local, kv_count, repeat, HD)
    )
    return spread.reshape(rows_local, kv_count * repeat * HD)


def body(query_proj, key_proj, value_proj, segment_ids, out_weight, residual, norm_gain):
    row_count = lax.axis_size("row")
    repeat = max(row_count // HK, 1)
    key_wide = widen_heads(key_proj, repeat)
    value_wide = widen_heads(value_proj, repeat)
    query_heads, key_heads, value_heads = (
        lax.all_to_all(query_proj, "row", split_axis=1, concat_axis=0, tiled=True),
        lax.all_to_all(key_wide, "row", split_axis=1, concat_axis=0, tiled=True),
        lax.all_to_all(value_wide, "row", split_axis=1, concat_axis=0, tiled=True),
    )
    attn = attend_local(query_heads, key_heads, value_heads, segment_ids[0])
    panel_rows = lax.all_gather(attn, "row", axis=1, tiled=True)
    projected = jnp.dot(
        panel_rows,
        lax.all_gather(out_weight, "col", axis=0, tiled=True),
        preferred_element_type=jnp.float32,
    )
    hidden_sum = residual.astype(jnp.float32) + projected
    squares = lax.psum(jnp.sum(hidden_sum * hidden_sum, axis=1), "row")
    scaled = lax.rsqrt(squares / D + jnp.float32(1e-05))
    normed = hidden_sum * scaled[:, None] * norm_gain[None, :]
    return (hidden_sum.astype(jnp.bfloat16), normed.astype(jnp.bfloat16))


def solution(mesh):
    placed = (
        P(("col", "row"), None),
        P(("col", "row"), None),
        P(("col", "row"), None),
        P("col", None),
        P("col", "row"),
        P("col", "row"),
        P("row"),
    )
    return jax.shard_map(
        body,
        mesh=mesh,
        in_specs=placed,
        out_specs=(P("col", "row"), P("col", "row")),
        check_vma=False,
    )
```

profile of v0, /device:TPU:0, one launch (start us, length us, event | category | flops | bytes accessed | tf_op | source)
XLA Modules:
  0.0 514.9 jit_solution(6233350073334996084)
XLA Ops:
  7.2 1.9 copy.42
  9.0 4.2 all-to-all-start.1
  13.2 1.9 copy.41
  15.1 6.9 %all-to-all-done.1 = bf16[512,2,256]{2,0,1:T(8,128)(2,1)S(1)} async-done(((bf16[512,2,256]{2,0,1:T(8,128)(2,1)}), bf16[512,2,256]{2,0,1:T(8,128)(2,1)S(1)}, u32[]{:S(2)}, u32[]{:S(2)}) %all-to-all-start.1) | async-done | bytes 524320 | tf_op jit(solution)/shard_map/all_to_all | solution.py:59
  22.0 3.5 all-to-all-start.2
  25.5 4.8 copy.40
  30.3 2.9 all-to-all-done.2
  33.1 5.6 %all-to-all-start = ((bf16[512,2,2048]{2,0,1:T(8,128)(2,1)}), bf16[512,2,2048]{2,0,1:T(8,128)(2,1)}, u32[]{:S(2)}, u32[]{:S(2)}) async-start(bf16[512,2,2048]{2,0,1:T(8,128)(2,1)} %bitcast.71), calls=%async_computation | async-start | bytes 8388608 | tf_op jit(solution)/shard_map/all_to_all | solution.py:58
  38.8 0.1 reshape.34
  39.0 0.9 copy.15
  40.0 0.9 copy.16
  40.9 44.1 %all-to-all-done = bf16[512,2,2048]{2,0,1:T(8,128)(2,1)} async-done(((bf16[512,2,2048]{2,0,1:T(8,128)(2,1)}), bf16[512,2,2048]{2,0,1:T(8,128)(2,1)}, u32[]{:S(2)}, u32[]{:S(2)}) %all-to-all-start) | async-done | bytes 4194336 | tf_op jit(solution)/shard_map/all_to_all | solution.py:58
  85.0 5.6 %copy.25 = bf16[128,8,16,128]{3,2,1,0:T(8,128)(2,1)} copy(bf16[128,8,16,128]{3,1,2,0:T(8,128)(2,1)} %bitcast.23) | data formatting | bytes 8388608
  90.6 74.1 %while.11 = (s32[]{:T(128)}, bf16[2,8,1024,128]{2,3,1,0:T(8,128)(2,1)}, bf16[2,8,1024,128]{3,1,0,2:T(8,128)(2,1)}, bf16[2,1024,128]{2,1,0:T(8,128)(2,1)}, bf16[2...) while((s32[]{:T(128)}, bf16[2,8,1024,128]{2,3,1,0:T(8,128)(2,1)}, ...), condition=%wide.region_3.4_spmd.clone, body=%wide.region_0.3_spmd.clone.sunk | while | flops 4350542848 | bytes 54072912 | solution.py:37
  90.6 1.7 constant_dynamic-slice_fusion.2
  92.3 0.6 fusion.52
  92.9 20.1 %fusion.53 = (f32[8,1024]{1,0:T(8,128)S(1)}, bf16[8,1024,1024]{1,2,0:T(8,128)(2,1)}) fusion(pred[1024,1024]{0,1:T(8,128)(4,1)S(1)} %fusion.52, bf16[1,8,1024,128]{3,1,0,2:T(8,128)(2,1)S(1)} %constant_dynamic-slice_fusion.2, bf16[2,1024,128]{2,1,0:T(8,128)(2,1)} %get-tuple-element.134, s32[]{:T(128)} %get-tuple-element.124), kind=kOutput, calls=%fused_computation.37.clone.1 | convolution fusion | flops 2197816320 | bytes 21266944 | tf_op jit(solution)/shard_map/while/body/eval_jaxpr/sub | solution.py:28
  113.1 10.1 %fusion.54 = bf16[1,8,1024,128]{3,2,1,0:T(8,128)(2,1)} fusion(f32[8,1024]{1,0:T(8,128)S(1)} %get-tuple-element.115, bf16[8,1024,1024]{1,2,0:T(8,128)(2,1)} %get-tuple-element.116, bf16[2,1024,128]{2,1,0:T(8,128)(2,1)} %get-tuple-element.135, s32[]{:T(128)} %get-tuple-element.124), kind=kOutput, calls=%fused_computation.16.clone.1 | convolution fusion | flops 2149580800 | bytes 19169792 | tf_op jit(solution)/shard_map/while/body/eval_jaxpr/gqk,kd->gqd/dot_general | solution.py:32
  123.2 2.9 copy.46
  126.0 1.6 constant_dynamic-update-slice_fusion.2
  127.6 1.7 constant_dynamic-slice_fusion.2
  129.4 0.6 fusion.52
  130.0 20.1 %fusion.53 = (f32[8,1024]{1,0:T(8,128)S(1)}, bf16[8,1024,1024]{1,2,0:T(8,128)(2,1)}) fusion(pred[1024,1024]{0,1:T(8,128)(4,1)S(1)} %fusion.52, bf16[1,8,1024,128]{3,1,0,2:T(8,128)(2,1)S(1)} %constant_dynamic-slice_fusion.2, bf16[2,1024,128]{2,1,0:T(8,128)(2,1)} %get-tuple-element.134, s32[]{:T(128)} %get-tuple-element.124), kind=kOutput, calls=%fused_computation.37.clone.1 | convolution fusion | flops 2197816320 | bytes 21266944 | tf_op jit(solution)/shard_map/while/body/eval_jaxpr/sub | solution.py:28
  150.1 10.1 %fusion.54 = bf16[1,8,1024,128]{3,2,1,0:T(8,128)(2,1)} fusion(f32[8,1024]{1,0:T(8,128)S(1)} %get-tuple-element.115, bf16[8,1024,1024]{1,2,0:T(8,128)(2,1)} %get-tuple-element.116, bf16[2,1024,128]{2,1,0:T(8,128)(2,1)} %get-tuple-element.135, s32[]{:T(128)} %get-tuple-element.124), kind=kOutput, calls=%fused_computation.16.clone.1 | convolution fusion | flops 2149580800 | bytes 19169792 | tf_op jit(solution)/shard_map/while/body/eval_jaxpr/gqk,kd->gqd/dot_general | solution.py:32
  160.2 2.9 copy.46
  163.1 1.6 constant_dynamic-update-slice_fusion.2
  164.8 0.7 all-gather.5.cloned.1.call-update
  165.5 103.3 %all-gather.3.cloned.1.call-done = bf16[1024,4096]{0,1:T(8,128)(2,1)} async-done(((bf16[1024,2048]{0,1:T(8,128)(2,1)}), bf16[1024,4096]{0,1:T(8,128)(2,1)}) %all-gather.3.cloned.1.call-update) | async-done | bytes 8388624 | tf_op jit(solution)/shard_map/all_gather | solution.py:63
  268.8 169.7 %all-gather.5.cloned.1.call-done = bf16[4096,4096]{1,0:T(8,128)(2,1)} async-done(((bf16[256,4096]{1,0:T(8,128)(2,1)}), bf16[4096,4096]{1,0:T(8,128)(2,1)}) %all-gather.5.cloned.1.call-update) | async-done | bytes 33554448 | tf_op jit(solution)/shard_map/all_gather | solution.py:66
  438.5 45.1 %multiply_reduce_fusion = (f32[1024]{0:T(1024)S(1)}, f32[1024,4096]{1,0:T(8,128)}) fusion(bf16[1024,4096]{0,1:T(8,128)(2,1)} %all-gather.3.cloned.1.call-done, bf16[4096,4096]{1,0:T(8,128)(2,1)} %all-gather.5.cloned.1.call-done, bf16[1024,4096]{1,0:T(8,128)(2,1)} %param.14), kind=kOutput, calls=%fused_computation.31 | convolution fusion | flops 34376515584 | bytes 67112960 | tf_op jit(solution)/shard_map/dot_general | solution.py:64
  483.6 4.9 psum.7
  488.5 19.5 %multiply_convert_fusion = (bf16[1024,4096]{1,0:T(8,128)(2,1)}, bf16[1024,4096]{1,0:T(8,128)(2,1)}) fusion(f32[1024,4096]{1,0:T(8,128)} %get-tuple-element.73, f32[4096]{0:T(1024)S(1)} %copy-done.1, f32[1024]{0:T(1024)S(1)} %add_rsqrt_fusion), kind=kLoop, calls=%fused_computation.30 | loop fusion | flops 16777216 | bytes 33574912 | tf_op jit(solution)/shard_map/convert_element_type | solution.py:73
  (10 shorter events, 0.2 us)
Async XLA Ops:
  9.0 12.9 %all-to-all-start.1 = ((bf16[512,2,256]{2,0,1:T(8,128)(2,1)}), bf16[512,2,256]{2,0,1:T(8,128)(2,1)S(1)}, u32[]{:S(2)}, u32[]{:S(2)}) async-start(bf16[512,2,256]{2,0,1:T(8,128)(2,1)} %bitcast.59), calls=%async_computation.1 | async-start | bytes 1048576 | tf_op jit(solution)/shard_map/all_to_all | solution.py:59
  22.0 11.2 %all-to-all-start.2 = ((bf16[512,2,256]{2,0,1:T(8,128)(2,1)}), bf16[512,2,256]{2,0,1:T(8,128)(2,1)S(1)}, u32[]{:S(2)}, u32[]{:S(2)}) async-start(bf16[512,2,256]{2,0,1:T(8,128)(2,1)} %bitcast.58), calls=%async_computation.2 | async-start | bytes 1048576 | tf_op jit(solution)/shard_map/all_to_all | solution.py:60
  33.1 51.8 %all-to-all-start = ((bf16[512,2,2048]{2,0,1:T(8,128)(2,1)}), bf16[512,2,2048]{2,0,1:T(8,128)(2,1)}, u32[]{:S(2)}, u32[]{:S(2)}) async-start(bf16[512,2,2048]{2,0,1:T(8,128)(2,1)} %bitcast.71), calls=%async_computation | async-start | bytes 8388608 | tf_op jit(solution)/shard_map/all_to_all | solution.py:58
  38.8 51.8 %copy-start = (s32[1,1024]{1,0:T(1,128)S(1)}, s32[1,1024]{1,0:T(1,128)}, u32[]{:S(2)}) copy-start(s32[1,1024]{1,0:T(1,128)} %param.12) | copy-start | bytes 12292
  38.8 230.0 %all-gather.3.cloned.1.call-start = ((), (), s32[]{:S(2)}) async-start(), calls=%async_computation.3 | async-start | bytes 12582912 | tf_op jit(solution)/shard_map/all_gather | solution.py:63
  164.7 273.8 %all-gather.5.cloned.1.call-start = ((), (), s32[]{:S(2)}) async-start(), calls=%async_computation.4 | async-start | bytes 35651584 | tf_op jit(solution)/shard_map/all_gather | solution.py:66
  165.5 323.1 %copy-start.1 = (f32[4096]{0:T(1024)S(1)}, f32[4096]{0:T(1024)}, u32[]{:S(2)}) copy-start(f32[4096]{0:T(1024)} %param.15) | copy-start | bytes 49156
Sparse Core Ops, SparseCore 0:
  164.9 103.9 all-gather.2
  270.4 168.0 all-gather.4
where the time goes:
time: 516 us; the launch traced here: 515 us
  waiting for transfers between devices  328 us (64%)
  matrix products  106 us (21%)
  local copies, waits for them, and re-layouts  28.5 us (6%)
  other arithmetic  20.7 us (4%)
  between operations  14.1 us (3%)
  starting transfers between devices  13.4 us (3%)
    all_gather x1, waiting for transfers between devices, body(): lax.all_gather(out_weight, 'col', axis=0, tiled=True)  170 us
    all_gather x1, waiting for transfers between devices, body(): panel_rows = lax.all_gather(attn, 'row', axis=1, tiled=True)  103 us
    dot_general x1, matrix products, body(): jnp.dot(panel_rows, lax.all_gather(out_weight, 'col', axis=0, tiled=True)...  45.1 us
    all_to_all x1, waiting for transfers between devices, body(): lax.all_to_all(query_proj, 'row', split_axis=1, concat_axis=0, tiled=True)  44.1 us
    sub x2, matrix products, one_group(): weights = jnp.where(allowed, jnp.exp(scores - peak), jnp.float32(0.0))  40.3 us
    dot_general x2, matrix products, one_group(): jnp.einsum('gqk,kd->gqd', probs, group_value, preferred_element_type=jnp....  20.2 us
    convert_element_type x1, other arithmetic, body(): return (hidden_sum.astype(jnp.bfloat16), normed.astype(jnp.bfloat16))  19.5 us
  transfers between devices with their start and end apart: 5, of which 5 were waited for; matrix products, arithmetic and copies ran while one was open for 2% of the time, Pallas kernels for 0%

commit v1 on v0

--- a/solution.py
+++ b/solution.py
@@ -6,6 +6,12 @@
 D = 8192
 HD = 128
 HK = 4
+
+
+def _save_indices(arr, d_out):
+    all_rows = list(arr.shape[1:])
+    all_rows[d_out] *= arr.shape[0]
+    return jnp.moveaxis(arr, 0, d_out).reshape(all_rows)
 
 
 def attend_local(query_heads, key_heads, value_heads, segment_row):
@@ -50,6 +56,26 @@
 
 
 def body(query_proj, key_proj, value_proj, segment_ids, out_weight, residual, norm_gain):
+
+    def press_heaps(vector, net_axis, where_dim):
+        how_many = jax.lax.axis_size(net_axis)
+        steps_seen = [(k, (k + 1) % how_many) for k in range(how_many)]
+        items = [(it, d) for d, it in steps_seen]
+        d_next, big = ([], [])
+        h = 0
+        while h < how_many - 1:
+            if h % 2 == 0:
+                d_next.append(
+                    jax.lax.ppermute(d_next[-1] if d_next else vector, net_axis, steps_seen)
+                )
+            else:
+                big.append(jax.lax.ppermute(big[-1] if big else vector, net_axis, items))
+            h += 1
+        state_now = jnp.stack([*d_next[::-1], vector, *big], axis=0)
+        reply = jax.lax.axis_index(net_axis) - len(d_next)
+        state_now = state_now[(jnp.arange(how_many) - reply) % how_many]
+        return _save_indices(state_now, where_dim)
+
     row_count = lax.axis_size("row")
     repeat = max(row_count // HK, 1)
     key_wide = widen_heads(key_proj, repeat)
@@ -62,9 +88,7 @@
     attn = attend_local(query_heads, key_heads, value_heads, segment_ids[0])
     panel_rows = lax.all_gather(attn, "row", axis=1, tiled=True)
     projected = jnp.dot(
-        panel_rows,
-        lax.all_gather(out_weight, "col", axis=0, tiled=True),
-        preferred_element_type=jnp.float32,
+        panel_rows, press_heaps(out_weight, "col", 0), preferred_element_type=jnp.float32
     )
     hidden_sum = residual.astype(jnp.float32) + projected
     squares = lax.psum(jnp.sum(hidden_sum * hidden_sum, axis=1), "row")

time: 516 us -> 566 us (1.097)
  waiting for transfers between devices: 328 us -> 139 us
  starting transfers between devices: 13.4 us -> 161 us
  local copies, waits for them, and re-layouts: 28.5 us -> 96.4 us
  other arithmetic: 20.7 us -> 44.2 us
    all_gather x1 -> x0, waiting for transfers between devices: 170 us -> none  [body(): lax.all_gather(out_weight, 'col', axis=0, tiled=True)]
    ppermute x0 -> x15, starting transfers between devices: none -> 148 us  [the longest x8 140 us: press_heaps(): jax.lax.ppermute(d_next[-1] if d_next else vector, net_axis, steps_seen)]
    all_gather x1, waiting for transfers between devices: 103 us -> 13.3 us  [body(): panel_rows = lax.all_gather(attn, 'row', axis=1, tiled=True)]
    ppermute x0 -> x15, waiting for transfers between devices: none -> 72.3 us  [the longest x8 70.7 us: press_heaps(): jax.lax.ppermute(d_next[-1] if d_next else vector, net_axis, steps_seen)]
    gather x0 -> x3, local copies, waits for them, and re-layouts: none -> 38.1 us  [press_heaps(): state_now = state_now[(jnp.arange(how_many) - reply) % how_many]]
    unnamed x7 -> x44, local copies, waits for them, and re-layouts: 7.38 us -> 34.6 us
    unnamed x0 -> x1, other arithmetic: none -> 22.8 us
  transfers between devices with their start and end apart: 5 -> 19, of which waited for: 5 -> 10; matrix products, arithmetic and copies ran while one was open for 2% -> 31% of each run, Pallas kernels for 0% -> 0%
where the time goes in v1:
time: 566 us; the launch traced here: 565 us
  starting transfers between devices  161 us (28%)
  waiting for transfers between devices  139 us (25%)
  matrix products  106 us (19%)
  local copies, waits for them, and re-layouts  96.4 us (17%)
  other arithmetic  44.2 us (8%)
  between operations  14.4 us (3%)
    ppermute x8, starting transfers between devices, press_heaps(): jax.lax.ppermute(d_next[-1] if d_next else vector, net_axis, steps_seen)  140 us
    ppermute x8, waiting for transfers between devices, press_heaps(): jax.lax.ppermute(d_next[-1] if d_next else vector, net_axis, steps_seen)  70.7 us
    dot_general x1, matrix products, body(): jnp.dot(panel_rows, press_heaps(out_weight, 'col', 0), preferred_element_...  45.1 us
    all_to_all x1, waiting for transfers between devices, body(): lax.all_to_all(query_proj, 'row', split_axis=1, concat_axis=0, tiled=True)  43 us
    sub x2, matrix products, one_group(): weights = jnp.where(allowed, jnp.exp(scores - peak), jnp.float32(0.0))  40.3 us
    gather x3, local copies, waits for them, and re-layouts, press_heaps(): state_now = state_now[(jnp.arange(how_many) - reply) % how_many]  38.1 us
    unnamed x44, local copies, waits for them, and re-layouts  34.6 us
    unnamed x1, other arithmetic  22.8 us
  transfers between devices with their start and end apart: 19, of which 10 were waited for; matrix products, arithmetic and copies ran while one was open for 31% of the time, Pallas kernels for 0%

profile of v1, /device:TPU:0, one launch (start us, length us, event | category | flops | bytes accessed | tf_op | source)
XLA Modules:
  0.0 565.2 jit_solution(454964540189847443)
XLA Ops:
  7.7 28.9 %collective-permute-done = bf16[256,4096]{1,0:T(8,128)(2,1)S(1)} collective-permute-done((bf16[256,4096]{1,0:T(8,128)(2,1)}, bf16[256,4096]{1,0:T(8,128)(2,1)S(1)}, u32[]{:S(2)}, u32[]{:S(2)}) %collective-permute-start) | collective-permute-done | bytes 2097184 | tf_op jit(solution)/shard_map/ppermute | solution.py:69
  37.9 4.4 collective-permute-start.8
  42.4 23.8 %collective-permute-done.1 = bf16[256,4096]{1,0:T(8,128)(2,1)S(1)} collective-permute-done((bf16[256,4096]{1,0:T(8,128)(2,1)S(1)}, bf16[256,4096]{1,0:T(8,128)(2,1)S(1)}, u32[]{:S(2)}, u32[]{:S(2)}) %collective-permute-start.1) | collective-permute-done | bytes 2097184 | tf_op jit(solution)/shard_map/ppermute | solution.py:69
  66.2 16.6 %collective-permute-start.2 = (bf16[256,4096]{1,0:T(8,128)(2,1)S(1)}, bf16[256,4096]{1,0:T(8,128)(2,1)S(1)}, u32[]{:S(2)}, u32[]{:S(2)}) collective-permute-start(bf16[256,4096]{1,0:T(8,128)(2,1)S(1)} %collective-permute-done.1), channel_id=1, source_target_pairs={{0,1},{1,2},{2,3},{3,4},{4,5},{5,6},{6,7},{7,8},{8,9},{9,10},{10,1... | collective-permute-start | bytes 6291464 | tf_op jit(solution)/shard_map/ppermute | solution.py:69
  84.1 10.4 %collective-permute-done.2 = bf16[256,4096]{1,0:T(8,128)(2,1)S(1)} collective-permute-done((bf16[256,4096]{1,0:T(8,128)(2,1)S(1)}, bf16[256,4096]{1,0:T(8,128)(2,1)S(1)}, u32[]{:S(2)}, u32[]{:S(2)}) %collective-permute-start.2) | collective-permute-done | bytes 2097184 | tf_op jit(solution)/shard_map/ppermute | solution.py:69
  94.5 36.2 %collective-permute-start.3 = (bf16[256,4096]{1,0:T(8,128)(2,1)S(1)}, bf16[256,4096]{1,0:T(8,128)(2,1)S(1)}, u32[]{:S(2)}, u32[]{:S(2)}) collective-permute-start(bf16[256,4096]{1,0:T(8,128)(2,1)S(1)} %collective-permute-done.2), channel_id=1, source_target_pairs={{0,1},{1,2},{2,3},{3,4},{4,5},{5,6},{6,7},{7,8},{8,9},{9,10},{10,1... | collective-permute-start | bytes 6291464 | tf_op jit(solution)/shard_map/ppermute | solution.py:69
  132.1 3.7 collective-permute-done.3
  135.8 42.1 %collective-permute-start.4 = (bf16[256,4096]{1,0:T(8,128)(2,1)S(1)}, bf16[256,4096]{1,0:T(8,128)(2,1)}, u32[]{:S(2)}, u32[]{:S(2)}) collective-permute-start(bf16[256,4096]{1,0:T(8,128)(2,1)S(1)} %collective-permute-done.3), channel_id=1, source_target_pairs={{0,1},{1,2},{2,3},{3,4},{4,5},{5,6},{6,7},{7,8},{8,9},{9,10},{10,1... | collective-permute-start | bytes 6291464 | tf_op jit(solution)/shard_map/ppermute | solution.py:69
  178.0 3.8 collective-permute-done.4
  181.8 43.3 %collective-permute-start.5 = (bf16[256,4096]{1,0:T(8,128)(2,1)}, bf16[256,4096]{1,0:T(8,128)(2,1)}, u32[]{:S(2)}, u32[]{:S(2)}) collective-permute-start(bf16[256,4096]{1,0:T(8,128)(2,1)} %collective-permute-done.4), channel_id=1, source_target_pairs={{0,1},{1,2},{2,3},{3,4},{4,5},{5,6},{6,7},{7,8},{8,9},{9,10},{10,1... | collective-permute-start | bytes 6291464 | tf_op jit(solution)/shard_map/ppermute | solution.py:69
  227.0 3.5 all-to-all-start.1
  232.4 5.8 %all-to-all-done.1 = bf16[512,2,256]{2,0,1:T(8,128)(2,1)S(1)} async-done(((bf16[512,2,256]{2,0,1:T(8,128)(2,1)}), bf16[512,2,256]{2,0,1:T(8,128)(2,1)S(1)}, u32[]{:S(2)}, u32[]{:S(2)}) %all-to-all-start.1) | async-done | bytes 524320 | tf_op jit(solution)/shard_map/all_to_all | solution.py:85
  238.2 3.5 all-to-all-start.2
  241.7 4.8 copy.40
  246.5 4.1 all-to-all-done.2
  250.6 5.6 all-to-all-start
  261.3 43.0 %all-to-all-done = bf16[512,2,2048]{2,0,1:T(8,128)(2,1)} async-done(((bf16[512,2,2048]{2,0,1:T(8,128)(2,1)}), bf16[512,2,2048]{2,0,1:T(8,128)(2,1)}, u32[]{:S(2)}, u32[]{:S(2)}) %all-to-all-start) | async-done | bytes 4194336 | tf_op jit(solution)/shard_map/all_to_all | solution.py:84
  304.4 5.6 copy.25
  310.5 74.3 %while.11 = (s32[]{:T(128)}, bf16[2,8,1024,128]{2,3,1,0:T(8,128)(2,1)}, bf16[2,8,1024,128]{3,1,0,2:T(8,128)(2,1)}, bf16[2,1024,128]{2,1,0:T(8,128)(2,1)}, bf16[2...) while((s32[]{:T(128)}, bf16[2,8,1024,128]{2,3,1,0:T(8,128)(2,1)}, ...), condition=%wide.region_3.4_spmd.clone, body=%wide.region_0.3_spmd.clone.sunk | while | flops 4350542848 | bytes 54072912 | solution.py:43
  312.8 20.2 %fusion.56 = (f32[8,1024]{1,0:T(8,128)S(1)}, bf16[8,1024,1024]{1,2,0:T(8,128)(2,1)}) fusion(pred[1024,1024]{0,1:T(8,128)(4,1)S(1)} %fusion.55, bf16[1,8,1024,128]{3,1,0,2:T(8,128)(2,1)S(1)} %constant_dynamic-slice_fusion.2, bf16[2,1024,128]{2,1,0:T(8,128)(2,1)} %get-tuple-element.136, s32[]{:T(128)} %get-tuple-element.126), kind=kOutput, calls=%fused_computation.63.clone.1 | convolution fusion | flops 2197816320 | bytes 21266944 | tf_op jit(solution)/shard_map/while/body/eval_jaxpr/sub | solution.py:34
  333.0 10.2 %fusion.57 = bf16[1,8,1024,128]{3,2,1,0:T(8,128)(2,1)} fusion(f32[8,1024]{1,0:T(8,128)S(1)} %get-tuple-element.117, bf16[8,1024,1024]{1,2,0:T(8,128)(2,1)} %get-tuple-element.118, bf16[2,1024,128]{2,1,0:T(8,128)(2,1)} %get-tuple-element.137, s32[]{:T(128)} %get-tuple-element.126), kind=kOutput, calls=%fused_computation.18.clone.1 | convolution fusion | flops 2149580800 | bytes 19169792 | tf_op jit(solution)/shard_map/while/body/eval_jaxpr/gqk,kd->gqd/dot_general | solution.py:38
  350.0 20.2 %fusion.56 = (f32[8,1024]{1,0:T(8,128)S(1)}, bf16[8,1024,1024]{1,2,0:T(8,128)(2,1)}) fusion(pred[1024,1024]{0,1:T(8,128)(4,1)S(1)} %fusion.55, bf16[1,8,1024,128]{3,1,0,2:T(8,128)(2,1)S(1)} %constant_dynamic-slice_fusion.2, bf16[2,1024,128]{2,1,0:T(8,128)(2,1)} %get-tuple-element.136, s32[]{:T(128)} %get-tuple-element.126), kind=kOutput, calls=%fused_computation.63.clone.1 | convolution fusion | flops 2197816320 | bytes 21266944 | tf_op jit(solution)/shard_map/while/body/eval_jaxpr/sub | solution.py:34
  370.1 10.2 %fusion.57 = bf16[1,8,1024,128]{3,2,1,0:T(8,128)(2,1)} fusion(f32[8,1024]{1,0:T(8,128)S(1)} %get-tuple-element.117, bf16[8,1024,1024]{1,2,0:T(8,128)(2,1)} %get-tuple-element.118, bf16[2,1024,128]{2,1,0:T(8,128)(2,1)} %get-tuple-element.137, s32[]{:T(128)} %get-tuple-element.126), kind=kOutput, calls=%fused_computation.18.clone.1 | convolution fusion | flops 2149580800 | bytes 19169792 | tf_op jit(solution)/shard_map/while/body/eval_jaxpr/gqk,kd->gqd/dot_general | solution.py:38
  384.8 4.1 collective-permute-start.14
  414.6 11.7 %fusion.42 = (bf16[16,256,2048]{2,1,0:T(8,128)(2,1)}, bf16[16,256,2048]{2,1,0:T(8,128)(2,1)}) fusion(bf16[16,256,4096]{2,1,0:T(8,128)(2,1)S(1)} %bitcast_dynamic-update-slice_fusion), kind=kLoop, calls=%fused_computation.64 | loop fusion | bytes 67108864 | tf_op jit(solution)/shard_map/gather | solution.py:76
  426.3 13.2 %gather_fusion = bf16[16,256,2048]{2,1,0:T(8,128)(2,1)} fusion(bf16[16,256,2048]{2,1,0:T(8,128)(2,1)} %get-tuple-element.70, s32[1024]{0:T(1024)} %pad_clamp_fusion), kind=kCustom, calls=%fused_computation | custom fusion | bytes 33554496 | tf_op jit(solution)/shard_map/gather | solution.py:76
  439.5 13.2 %gather_fusion.1 = bf16[16,256,2048]{2,1,0:T(8,128)(2,1)} fusion(bf16[16,256,2048]{2,1,0:T(8,128)(2,1)} %get-tuple-element.71, s32[1024]{0:T(1024)} %pad_clamp_fusion), kind=kCustom, calls=%fused_computation.1 | custom fusion | bytes 33554496 | tf_op jit(solution)/shard_map/gather | solution.py:76
  452.6 22.8 %pad_maximum_fusion = bf16[16,256,4096]{2,1,0:T(8,128)(2,1)} fusion(bf16[16,256,2048]{2,1,0:T(8,128)(2,1)} %gather_fusion.1, bf16[16,256,2048]{2,1,0:T(8,128)(2,1)} %gather_fusion), kind=kLoop, calls=%fused_computation.32 | loop fusion | flops 67108864 | bytes 67108864
  475.4 13.3 %all-gather.2.cloned.1.call-done = bf16[1024,4096]{0,1:T(8,128)(2,1)} async-done(((bf16[1024,2048]{0,1:T(8,128)(2,1)}), bf16[1024,4096]{0,1:T(8,128)(2,1)}) %all-gather.2.cloned.1.call-update) | async-done | bytes 8388624 | tf_op jit(solution)/shard_map/all_gather | solution.py:89
  488.8 45.1 %multiply_reduce_fusion = (f32[1024]{0:T(1024)S(1)}, f32[1024,4096]{1,0:T(8,128)}) fusion(bf16[1024,4096]{0,1:T(8,128)(2,1)} %all-gather.2.cloned.1.call-done, bf16[4096,4096]{1,0:T(8,128)(2,1)} %bitcast.106, bf16[1024,4096]{1,0:T(8,128)(2,1)} %param.14), kind=kOutput, calls=%fused_computation.34 | convolution fusion | flops 34376515584 | bytes 67112960 | tf_op jit(solution)/shard_map/dot_general | solution.py:90
  533.9 4.9 psum.7
  538.8 19.6 %multiply_convert_fusion = (bf16[1024,4096]{1,0:T(8,128)(2,1)}, bf16[1024,4096]{1,0:T(8,128)(2,1)}) fusion(f32[1024,4096]{1,0:T(8,128)} %get-tuple-element.75, f32[4096]{0:T(1024)S(1)} %copy-done.12, f32[1024]{0:T(1024)S(1)} %add_rsqrt_fusion), kind=kLoop, calls=%fused_computation.33 | loop fusion | flops 16777216 | bytes 33574912 | tf_op jit(solution)/shard_map/convert_element_type | solution.py:97
  (81 shorter events, 53.1 us)
Async XLA Ops:
  7.2 29.4 %collective-permute-start = (bf16[256,4096]{1,0:T(8,128)(2,1)}, bf16[256,4096]{1,0:T(8,128)(2,1)S(1)}, u32[]{:S(2)}, u32[]{:S(2)}) collective-permute-start(bf16[256,4096]{1,0:T(8,128)(2,1)} %param.13), channel_id=1, source_target_pairs={{0,1},{1,2},{2,3},{3,4},{4,5},{5,6},{6,7},{7,8},{8,9},{9,10},{10,1... | collective-permute-start | bytes 6291464 | tf_op jit(solution)/shard_map/ppermute | solution.py:69
  36.6 1.4 copy-start.1
  37.9 28.3 %collective-permute-start.1 = (bf16[256,4096]{1,0:T(8,128)(2,1)S(1)}, bf16[256,4096]{1,0:T(8,128)(2,1)S(1)}, u32[]{:S(2)}, u32[]{:S(2)}) collective-permute-start(bf16[256,4096]{1,0:T(8,128)(2,1)S(1)} %collective-permute-done), channel_id=1, source_target_pairs={{0,1},{1,2},{2,3},{3,4},{4,5},{5,6},{6,7},{7,8},{8,9},{9,10},{10,1... | collective-permute-start | bytes 6291464 | tf_op jit(solution)/shard_map/ppermute | solution.py:69
  37.9 44.8 %collective-permute-start.8 = (bf16[256,4096]{1,0:T(8,128)(2,1)}, bf16[256,4096]{1,0:T(8,128)(2,1)S(1)}, u32[]{:S(2)}, u32[]{:S(2)}) collective-permute-start(bf16[256,4096]{1,0:T(8,128)(2,1)} %param.13), channel_id=1, source_target_pairs={{1,0},{2,1},{3,2},{4,3},{5,4},{6,5},{7,6},{8,7},{9,8},{10,9},{11,1... | collective-permute-start | bytes 6291464 | tf_op jit(solution)/shard_map/ppermute | solution.py:72
  66.2 64.5 %copy-start.5 = (bf16[256,4096]{1,0:T(8,128)(2,1)}, bf16[256,4096]{1,0:T(8,128)(2,1)S(1)}, u32[]{:S(2)}) copy-start(bf16[256,4096]{1,0:T(8,128)(2,1)S(1)} %collective-permute-done.1) | copy-start | bytes 6291460
  66.2 28.3 %collective-permute-start.2 = (bf16[256,4096]{1,0:T(8,128)(2,1)S(1)}, bf16[256,4096]{1,0:T(8,128)(2,1)S(1)}, u32[]{:S(2)}, u32[]{:S(2)}) collective-permute-start(bf16[256,4096]{1,0:T(8,128)(2,1)S(1)} %collective-permute-done.1), channel_id=1, source_target_pairs={{0,1},{1,2},{2,3},{3,4},{4,5},{5,6},{6,7},{7,8},{8,9},{9,10},{10,1... | collective-permute-start | bytes 6291464 | tf_op jit(solution)/shard_map/ppermute | solution.py:69
  82.8 1.3 copy-start.3
  84.1 46.6 %collective-permute-start.9 = (bf16[256,4096]{1,0:T(8,128)(2,1)S(1)}, bf16[256,4096]{1,0:T(8,128)(2,1)S(1)}, u32[]{:S(2)}, u32[]{:S(2)}) collective-permute-start(bf16[256,4096]{1,0:T(8,128)(2,1)S(1)} %collective-permute-done.8), channel_id=1, source_target_pairs={{1,0},{2,1},{3,2},{4,3},{5,4},{6,5},{7,6},{8,7},{9,8},{10,9},{11,1... | collective-permute-start | bytes 6291464 | tf_op jit(solution)/shard_map/ppermute | solution.py:72
  94.5 83.5 %copy-start.8 = (bf16[256,4096]{1,0:T(8,128)(2,1)}, bf16[256,4096]{1,0:T(8,128)(2,1)S(1)}, u32[]{:S(2)}) copy-start(bf16[256,4096]{1,0:T(8,128)(2,1)S(1)} %collective-permute-done.2) | copy-start | bytes 6291460
  94.5 41.3 %collective-permute-start.3 = (bf16[256,4096]{1,0:T(8,128)(2,1)S(1)}, bf16[256,4096]{1,0:T(8,128)(2,1)S(1)}, u32[]{:S(2)}, u32[]{:S(2)}) collective-permute-start(bf16[256,4096]{1,0:T(8,128)(2,1)S(1)} %collective-permute-done.2), channel_id=1, source_target_pairs={{0,1},{1,2},{2,3},{3,4},{4,5},{5,6},{6,7},{7,8},{8,9},{9,10},{10,1... | collective-permute-start | bytes 6291464 | tf_op jit(solution)/shard_map/ppermute | solution.py:69
  130.7 1.4 copy-start.7
  130.7 47.2 %collective-permute-start.10 = (bf16[256,4096]{1,0:T(8,128)(2,1)S(1)}, bf16[256,4096]{1,0:T(8,128)(2,1)S(1)}, u32[]{:S(2)}, u32[]{:S(2)}) collective-permute-start(bf16[256,4096]{1,0:T(8,128)(2,1)S(1)} %collective-permute-done.9), channel_id=1, source_target_pairs={{1,0},{2,1},{3,2},{4,3},{5,4},{6,5},{7,6},{8,7},{9,8},{10,9},{11,1... | collective-permute-start | bytes 6291464 | tf_op jit(solution)/shard_map/ppermute | solution.py:72
  135.8 42.2 %copy-start.10 = (bf16[256,4096]{1,0:T(8,128)(2,1)}, bf16[256,4096]{1,0:T(8,128)(2,1)S(1)}, u32[]{:S(2)}) copy-start(bf16[256,4096]{1,0:T(8,128)(2,1)S(1)} %collective-permute-done.3) | copy-start | bytes 6291460
  135.8 46.0 %collective-permute-start.4 = (bf16[256,4096]{1,0:T(8,128)(2,1)S(1)}, bf16[256,4096]{1,0:T(8,128)(2,1)}, u32[]{:S(2)}, u32[]{:S(2)}) collective-permute-start(bf16[256,4096]{1,0:T(8,128)(2,1)S(1)} %collective-permute-done.3), channel_id=1, source_target_pairs={{0,1},{1,2},{2,3},{3,4},{4,5},{5,6},{6,7},{7,8},{8,9},{9,10},{10,1... | collective-permute-start | bytes 6291464 | tf_op jit(solution)/shard_map/ppermute | solution.py:69
  177.9 132.0 %copy-start.9 = (bf16[256,4096]{1,0:T(8,128)(2,1)}, bf16[256,4096]{1,0:T(8,128)(2,1)S(1)}, u32[]{:S(2)}) copy-start(bf16[256,4096]{1,0:T(8,128)(2,1)S(1)} %collective-permute-done.10) | copy-start | bytes 6291460
  177.9 78.4 %collective-permute-start.11 = (bf16[256,4096]{1,0:T(8,128)(2,1)S(1)}, bf16[256,4096]{1,0:T(8,128)(2,1)}, u32[]{:S(2)}, u32[]{:S(2)}) collective-permute-start(bf16[256,4096]{1,0:T(8,128)(2,1)S(1)} %collective-permute-done.10), channel_id=1, source_target_pairs={{1,0},{2,1},{3,2},{4,3},{5,4},{6,5},{7,6},{8,7},{9,8},{10,9},{11,1... | collective-permute-start | bytes 6291464 | tf_op jit(solution)/shard_map/ppermute | solution.py:72
  181.8 74.5 %collective-permute-start.5 = (bf16[256,4096]{1,0:T(8,128)(2,1)}, bf16[256,4096]{1,0:T(8,128)(2,1)}, u32[]{:S(2)}, u32[]{:S(2)}) collective-permute-start(bf16[256,4096]{1,0:T(8,128)(2,1)} %collective-permute-done.4), channel_id=1, source_target_pairs={{0,1},{1,2},{2,3},{3,4},{4,5},{5,6},{6,7},{7,8},{8,9},{9,10},{10,1... | collective-permute-start | bytes 6291464 | tf_op jit(solution)/shard_map/ppermute | solution.py:69
  225.1 85.4 %copy-start.11 = (s32[1,1024]{1,0:T(1,128)S(1)}, s32[1,1024]{1,0:T(1,128)}, u32[]{:S(2)}) copy-start(s32[1,1024]{1,0:T(1,128)} %param.12) | copy-start | bytes 12292
  227.0 11.2 %all-to-all-start.1 = ((bf16[512,2,256]{2,0,1:T(8,128)(2,1)}), bf16[512,2,256]{2,0,1:T(8,128)(2,1)S(1)}, u32[]{:S(2)}, u32[]{:S(2)}) async-start(bf16[512,2,256]{2,0,1:T(8,128)(2,1)} %bitcast.94), calls=%async_computation.1 | async-start | bytes 1048576 | tf_op jit(solution)/shard_map/all_to_all | solution.py:85
  238.2 12.4 %all-to-all-start.2 = ((bf16[512,2,256]{2,0,1:T(8,128)(2,1)}), bf16[512,2,256]{2,0,1:T(8,128)(2,1)S(1)}, u32[]{:S(2)}, u32[]{:S(2)}) async-start(bf16[512,2,256]{2,0,1:T(8,128)(2,1)} %bitcast.112), calls=%async_computation.2 | async-start | bytes 1048576 | tf_op jit(solution)/shard_map/all_to_all | solution.py:86
  250.6 53.7 %all-to-all-start = ((bf16[512,2,2048]{2,0,1:T(8,128)(2,1)}), bf16[512,2,2048]{2,0,1:T(8,128)(2,1)}, u32[]{:S(2)}, u32[]{:S(2)}) async-start(bf16[512,2,2048]{2,0,1:T(8,128)(2,1)} %bitcast.107), calls=%async_computation | async-start | bytes 8388608 | tf_op jit(solution)/shard_map/all_to_all | solution.py:84
  256.2 232.5 %all-gather.2.cloned.1.call-start = ((), (), s32[]{:S(2)}) async-start(), calls=%async_computation.3 | async-start | bytes 12582912 | tf_op jit(solution)/shard_map/all_gather | solution.py:89
  256.3 53.7 %collective-permute-start.12 = (bf16[256,4096]{1,0:T(8,128)(2,1)}, bf16[256,4096]{1,0:T(8,128)(2,1)}, u32[]{:S(2)}, u32[]{:S(2)}) collective-permute-start(bf16[256,4096]{1,0:T(8,128)(2,1)} %collective-permute-done.11), channel_id=1, source_target_pairs={{1,0},{2,1},{3,2},{4,3},{5,4},{6,5},{7,6},{8,7},{9,8},{10,9},{11,1... | collective-permute-start | bytes 6291464 | tf_op jit(solution)/shard_map/ppermute | solution.py:72
  256.4 53.6 %collective-permute-start.6 = (bf16[256,4096]{1,0:T(8,128)(2,1)}, bf16[256,4096]{1,0:T(8,128)(2,1)}, u32[]{:S(2)}, u32[]{:S(2)}) collective-permute-start(bf16[256,4096]{1,0:T(8,128)(2,1)} %collective-permute-done.5), channel_id=1, source_target_pairs={{0,1},{1,2},{2,3},{3,4},{4,5},{5,6},{6,7},{7,8},{8,9},{9,10},{10,1... | collective-permute-start | bytes 6291464 | tf_op jit(solution)/shard_map/ppermute | solution.py:69
  310.0 74.9 %collective-permute-start.13 = (bf16[256,4096]{1,0:T(8,128)(2,1)}, bf16[256,4096]{1,0:T(8,128)(2,1)}, u32[]{:S(2)}, u32[]{:S(2)}) collective-permute-start(bf16[256,4096]{1,0:T(8,128)(2,1)} %collective-permute-done.12), channel_id=1, source_target_pairs={{1,0},{2,1},{3,2},{4,3},{5,4},{6,5},{7,6},{8,7},{9,8},{10,9},{11,1... | collective-permute-start | bytes 6291464 | tf_op jit(solution)/shard_map/ppermute | solution.py:72
  310.0 78.9 %collective-permute-start.7 = (bf16[256,4096]{1,0:T(8,128)(2,1)}, bf16[256,4096]{1,0:T(8,128)(2,1)}, u32[]{:S(2)}, u32[]{:S(2)}) collective-permute-start(bf16[256,4096]{1,0:T(8,128)(2,1)} %collective-permute-done.6), channel_id=1, source_target_pairs={{0,1},{1,2},{2,3},{3,4},{4,5},{5,6},{6,7},{7,8},{8,9},{9,10},{10,1... | collective-permute-start | bytes 6291464 | tf_op jit(solution)/shard_map/ppermute | solution.py:69
  384.8 16.5 %copy-start.6 = (bf16[256,4096]{1,0:T(8,128)(2,1)S(1)}, bf16[256,4096]{1,0:T(8,128)(2,1)}, u32[]{:S(2)}) copy-start(bf16[256,4096]{1,0:T(8,128)(2,1)} %copy-done.5) | copy-start | bytes 6291460
  384.8 16.7 %copy-start.2 = (bf16[256,4096]{1,0:T(8,128)(2,1)S(1)}, bf16[256,4096]{1,0:T(8,128)(2,1)}, u32[]{:S(2)}) copy-start(bf16[256,4096]{1,0:T(8,128)(2,1)} %copy-done.1) | copy-start | bytes 6291460
  384.8 16.8 %copy-start = (bf16[256,4096]{1,0:T(8,128)(2,1)S(1)}, bf16[256,4096]{1,0:T(8,128)(2,1)}, u32[]{:S(2)}) copy-start(bf16[256,4096]{1,0:T(8,128)(2,1)} %param.13) | copy-start | bytes 6291460
  384.8 27.9 %collective-permute-start.14 = (bf16[256,4096]{1,0:T(8,128)(2,1)}, bf16[256,4096]{1,0:T(8,128)(2,1)}, u32[]{:S(2)}, u32[]{:S(2)}) collective-permute-start(bf16[256,4096]{1,0:T(8,128)(2,1)} %collective-permute-done.13), channel_id=1, source_target_pairs={{1,0},{2,1},{3,2},{4,3},{5,4},{6,5},{7,6},{8,7},{9,8},{10,9},{11,1... | collective-permute-start | bytes 6291464 | tf_op jit(solution)/shard_map/ppermute | solution.py:72
  390.7 11.1 %copy-start.4 = (bf16[256,4096]{1,0:T(8,128)(2,1)S(1)}, bf16[256,4096]{1,0:T(8,128)(2,1)}, u32[]{:S(2)}) copy-start(bf16[256,4096]{1,0:T(8,128)(2,1)} %copy-done.3) | copy-start | bytes 6291460
  488.8 50.0 %copy-start.12 = (f32[4096]{0:T(1024)S(1)}, f32[4096]{0:T(1024)}, u32[]{:S(2)}) copy-start(f32[4096]{0:T(1024)} %param.15) | copy-start | bytes 49156
Sparse Core Ops, SparseCore 0:
  384.9 103.8 all-gather.1
